TPU v7x, 32 devices: a whole 2x2x4 slice. The times are simulated.
32 devices in a mesh: row: 4 (over y, x), col: 8 (over z, core).
Axes of the slice: x: 2, y: 2, z: 4, core: 2. Of those that a mesh axis runs over, the one named last changes fastest.
Arguments:
- boundary_start: float32 [16384, 128], P('row'), may hold values from -6 to 6
- volume_start: float32 [256, 512, 128], P(('row', 'col')), may hold values from -6 to 6
- diag_part: float32 [16384], P(('row', 'col')), may hold values from 1 to 2
- incident: float32 [16384, 128], P(('row', 'col')), may hold values from -6 to 6
- kernel: float32 [16384, 16384], P('row', 'col'), may hold values from -0.015625 to 0.015625
- elem_mats: float32 [256, 512, 512], P(('row', 'col')), may hold values from -0.078125 to 0.078125
- trace_owner: int32 [16384, 1], replicated, may hold values from 0 to 31; in each aligned block of 512 rows (0 to 511, 512 to 1023, ...) at most 32 rows name the same one
- trace_slot: int32 [16384], replicated, may hold values from 0 to 4095
- return_owner: int32 [16384, 1], replicated, may hold values from 0 to 31; in each aligned block of 512 rows (0 to 511, 512 to 1023, ...) at most 32 rows name the same one
- return_slot: int32 [16384], replicated, may hold values from 0 to 4095
- face_match: int32 [256, 64], P(('row', 'col')), may hold values from 0 to 63, each once within a row
Outputs:
- boundary_final: float32 [16384, 128], P('row')
- volume_final: float32 [256, 512, 128], P(('row', 'col'))
Inputs may be any that keep to these rules, and one draw needn't show every extreme that they name: `trace_owner`: in each aligned block of 512 boundary rows (the rows of one device), no device is named more than 32 times; some device is named exactly 32 times in some block. `return_owner`: in each aligned block of 512 boundary rows (the rows of one device), no device is named more than 32 times; some device is named exactly 32 times in some block. `face_match`: each row is a permutation of 0 to 63.
All inputs are finite; a program needn't handle non-finite values.
Results may differ from a plain program's by a relative error of at most 0.0001.
Values sent between devices are 32-bit elements; how exact they have to be, the bound alone decides.
A program may use at most 128 MiB of HBM per device.

v0:
```python
import jax
import jax.numpy as jnp
from jax import lax
from jax.sharding import PartitionSpec as P

ITERS = 3
boundary_step = 0.5
volume_step = 0.6
face_weight = 0.5


def passed_along(block, axis, distance):
    devices = range(lax.axis_size(axis))
    route = [(i - distance, i) for i in devices if i - distance in devices]
    return lax.ppermute(block, axis, route)


def spread(block, axis, holder):
    block = jnp.where(lax.axis_index(axis) == holder, block, jnp.zeros_like(block))
    return lax.psum(block, axis)


def slot_rank(owners):
    row_total = owners.shape[0]
    same_owner = owners[:, None] == owners[None, :]
    positions = jnp.arange(row_total, dtype=jnp.int32)
    earlier = positions[None, :] < positions[:, None]
    return jnp.sum((same_owner & earlier).astype(jnp.int32), axis=1)


def send_plan(owners, rank_rows, devices, capacity):
    positions = jnp.arange(owners.shape[0], dtype=jnp.int32)
    targets = jnp.arange(devices, dtype=jnp.int32)
    places = jnp.arange(capacity, dtype=jnp.int32)
    select = (owners[None, None, :] == targets[:, None, None]) & (
        rank_rows[None, None, :] == places[None, :, None]
    )
    index = jnp.sum(jnp.where(select, positions[None, None, :], 0), axis=2)
    valid_slot = jnp.any(select, axis=2)
    return (index, valid_slot)


def block_plan(owner_blocks, slot_blocks, device_self, capacity):
    mine_rows = owner_blocks == device_self
    rank_rows = jnp.cumsum(mine_rows.astype(jnp.int32), axis=1) - 1
    places = jnp.arange(capacity, dtype=jnp.int32)
    select = mine_rows[:, None, :] & (rank_rows[:, None, :] == places[None, :, None])
    index = jnp.sum(jnp.where(select, slot_blocks[:, None, :], 0), axis=2)
    valid_slot = jnp.any(select, axis=2)
    return (index, valid_slot)


def shards(
    boundary_start,
    volume_start,
    diag_part,
    incident,
    kernel,
    elem_mats,
    trace_owner,
    trace_slot,
    return_owner,
    return_slot,
    face_match,
):
    highest = lax.Precision.HIGHEST
    devices = lax.axis_size(("row", "col"))
    row_devices = lax.axis_size("row")
    col_devices = lax.axis_size("col")
    device_self = lax.axis_index(("row", "col"))
    col_index = lax.axis_index("col")
    total_rows = trace_slot.shape[0]
    share_rows = total_rows // devices
    capacity = max(2, 2 * share_rows // devices)
    panel_length = total_rows // col_devices
    per_panel = col_devices // row_devices
    elem_count, node_count, columns = volume_start.shape
    face_count = face_match.shape[1]
    trace_blocks = trace_owner[:, 0].reshape(devices, share_rows)
    trace_slots = trace_slot.reshape(devices, share_rows)
    return_blocks = return_owner[:, 0].reshape(devices, share_rows)
    return_slots = return_slot.reshape(devices, share_rows)
    trace_send, trace_send_ok = block_plan(trace_blocks, trace_slots, device_self, capacity)
    own_trace = lax.dynamic_index_in_dim(trace_blocks, device_self, 0, keepdims=False)
    trace_pick = own_trace * capacity + slot_rank(own_trace)
    own_return = lax.dynamic_index_in_dim(return_blocks, device_self, 0, keepdims=False)
    flux_send, flux_send_ok = send_plan(own_return, slot_rank(own_return), devices, capacity)
    flux_take, flux_take_ok = block_plan(return_blocks, return_slots, device_self, capacity)
    panel_current = boundary_start
    volume_field = volume_start
    for sweep_index in range(ITERS):
        share_current = lax.dynamic_slice_in_dim(
            panel_current, col_index * share_rows, share_rows, 0
        )
        volume_flat = volume_field.reshape(elem_count * node_count, columns)
        outgoing = jnp.where(trace_send_ok[:, :, None], volume_flat[trace_send], 0.0)
        arrived = lax.all_to_all(outgoing, ("row", "col"), split_axis=0, concat_axis=0, tiled=True)
        traced = arrived.reshape(devices * capacity, columns)[trace_pick]
        leaving = jnp.where(flux_send_ok[:, :, None], share_current[flux_send], 0.0)
        landed = lax.all_to_all(leaving, ("row", "col"), split_axis=0, concat_axis=0, tiled=True)
        landed_rows = jnp.where(flux_take_ok[:, :, None], landed, 0.0).reshape(
            devices * capacity, columns
        )
        flux_field = (
            jnp.zeros_like(volume_flat)
            .at[flux_take.reshape(-1)]
            .add(landed_rows)
            .reshape(volume_field.shape)
        )
        lower_faces = passed_along(volume_field[:, node_count - face_count :, :], ("row", "col"), 1)
        matched = jax.vmap(lambda face_rows, face_order: face_rows[face_order])(
            lower_faces, face_match
        )
        half_panel = lax.dynamic_slice_in_dim(
            panel_current, col_index % per_panel * panel_length, panel_length, 0
        )
        column_values = spread(half_panel, "row", col_index // per_panel)
        local_term = diag_part[:, None] * share_current - incident - traced
        partial_value = jnp.dot(
            kernel, column_values, precision=highest, preferred_element_type=jnp.float32
        )
        row_start = col_index * share_rows
        own_part = lax.dynamic_slice_in_dim(partial_value, row_start, share_rows, 0) + local_term
        partial_value = lax.dynamic_update_slice_in_dim(partial_value, own_part, row_start, 0)
        residual = lax.psum(partial_value, "col")
        panel_current = panel_current - boundary_step * residual
        applied = jnp.einsum("enm,emr->enr", elem_mats, volume_field, precision=highest)
        updated = volume_field - volume_step * (volume_field + applied - flux_field)
        volume_field = updated.at[:, :face_count, :].add(volume_step * face_weight * matched)
    return (panel_current, volume_field)


def solution(mesh):
    placed = (
        P("row", None),
        P(("row", "col"), None, None),
        P(("row", "col")),
        P(("row", "col"), None),
        P("row", "col"),
        P(("row", "col"), None, None),
        P(),
        P(),
        P(),
        P(),
        P(("row", "col"), None),
    )
    return jax.shard_map(
        shards,
        mesh=mesh,
        in_specs=placed,
        out_specs=(P("row", None), P(("row", "col"), None, None)),
        check_vma=False,
    )
```

profile of v0, /device:TPU:0, one launch (start us, length us, event | category | flops | bytes accessed | tf_op | source)
XLA Modules:
  0.0 601.1 jit_solution(13699476681869330466)
XLA Ops:
  20.9 7.3 %all-to-all-start = ((f32[32,32,128]{2,1,0:T(8,128)}), f32[32,32,128]{2,1,0:T(8,128)S(1)}, u32[]{:S(2)}, u32[]{:S(2)}) async-start(f32[32,32,128]{2,1,0:T(8,128)} %broadcast_select_fusion.8), calls=%async_computation | async-start | bytes 1048576 | tf_op jit(solution)/shard_map/all_to_all | solution.py:97
  36.1 8.7 %all-to-all-done = f32[32,32,128]{2,1,0:T(8,128)S(1)} async-done(((f32[32,32,128]{2,1,0:T(8,128)}), f32[32,32,128]{2,1,0:T(8,128)S(1)}, u32[]{:S(2)}, u32[]{:S(2)}) %all-to-all-start) | async-done | bytes 524320 | tf_op jit(solution)/shard_map/all_to_all | solution.py:97
  46.0 23.2 %all-reduce.7.cloned.1.call-done = f32[2048,128]{0,1:T(8,128)} async-done(((f32[2048,128]{0,1:T(8,128)}), f32[2048,128]{0,1:T(8,128)}) %all-reduce.7.cloned.1.call-update) | async-done | bytes 1048592 | tf_op jit(solution)/shard_map/psum | solution.py:20
  69.2 38.4 %fusion.29 = f32[128,4096]{1,0:T(8,128)S(1)} fusion(f32[2048,128]{0,1:T(8,128)} %all-reduce.7.cloned.1.call-done, f32[4096,2048]{1,0:T(8,128)} %param.21), kind=kOutput, calls=%fused_computation.106 | convolution fusion | flops 12884901888 | bytes 36700160 | tf_op jit(solution)/shard_map/dot_general | solution.py:119
  114.6 4.6 all-to-all-start.1
  124.7 10.8 %all-to-all-done.1 = f32[32,32,128]{2,1,0:T(8,128)S(1)} async-done(((f32[32,32,128]{2,1,0:T(8,128)}), f32[32,32,128]{2,1,0:T(8,128)S(1)}, u32[]{:S(2)}, u32[]{:S(2)}) %all-to-all-start.1) | async-done | bytes 524320 | tf_op jit(solution)/shard_map/all_to_all | solution.py:100
  135.7 8.0 %scatter_custom_fusion = f32[4096,128]{1,0:T(8,128)} fusion(s32[1024]{0:T(1024)S(1)} %bitcast.132, f32[1024,128]{1,0:T(8,128)S(1)} %bitcast.123, f32[]{:T(128)} %constant.143.clone.1), kind=kCustom, calls=%fused_computation.44 | custom fusion | flops 131072 | bytes 2097156 | tf_op jit(solution)/shard_map/scatter-add | solution.py:107
  143.7 11.2 %multiply_subtract_fusion.2 = f32[8,512,128]{2,1,0:T(8,128)S(1)} fusion(f32[8,512,128]{2,1,0:T(8,128)} %param.18, f32[8,512,128]{2,1,0:T(8,128)} %bitcast.112, f32[8,512,512]{2,1,0:T(8,128)} %param.22), kind=kOutput, calls=%fused_computation.28 | convolution fusion | flops 3223322624 | bytes 14680064 | tf_op jit(solution)/shard_map/enm,emr->enr/dot_general | solution.py:127
  157.8 33.4 %all-reduce.9.cloned.1.call-done = f32[4096,128]{0,1:T(8,128)} async-done(((f32[4096,128]{0,1:T(8,128)}), f32[4096,128]{0,1:T(8,128)}) %all-reduce.9.cloned.1.call-update) | async-done | bytes 2097168 | tf_op jit(solution)/shard_map/psum | solution.py:125
  196.2 20.6 %all_to_all.30 = f32[32,32,128]{2,1,0:T(8,128)S(1)} all-to-all(f32[32,32,128]{2,1,0:T(8,128)S(1)} %broadcast_select_fusion.5), channel_id=1, replica_groups=mesh['row'=4,'col'=8] {'row','col'}, dimensions={0} | all-to-all | bytes 1048576 | tf_op jit(solution)/shard_map/all_to_all | solution.py:97
  218.1 35.8 %all-reduce.11.cloned.1.call-done = f32[2048,128]{0,1:T(8,128)} async-done(((f32[2048,128]{0,1:T(8,128)}), f32[2048,128]{0,1:T(8,128)}) %all-reduce.11.cloned.1.call-update) | async-done | bytes 1048592 | tf_op jit(solution)/shard_map/psum | solution.py:20
  253.9 39.2 %fusion.30 = f32[128,4096]{1,0:T(8,128)} fusion(f32[2048,128]{0,1:T(8,128)} %all-reduce.11.cloned.1.call-done, f32[4096,2048]{1,0:T(8,128)} %param.21), kind=kOutput, calls=%fused_computation.107 | convolution fusion | flops 12884901888 | bytes 36700160 | tf_op jit(solution)/shard_map/dot_general | solution.py:119
  312.8 9.4 %all-to-all-done.3 = f32[32,32,128]{2,1,0:T(8,128)S(1)} async-done(((f32[32,32,128]{2,1,0:T(8,128)}), f32[32,32,128]{2,1,0:T(8,128)S(1)}, u32[]{:S(2)}, u32[]{:S(2)}) %all-to-all-start.3) | async-done | bytes 524320 | tf_op jit(solution)/shard_map/all_to_all | solution.py:100
  322.4 8.1 %scatter_custom_fusion.1 = f32[4096,128]{1,0:T(8,128)} fusion(s32[1024]{0:T(1024)S(1)} %bitcast.133, f32[1024,128]{1,0:T(8,128)S(1)} %bitcast.124, f32[]{:T(128)} %constant.143.clone.1), kind=kCustom, calls=%fused_computation.42 | custom fusion | flops 131072 | bytes 2097156 | tf_op jit(solution)/shard_map/scatter-add | solution.py:107
  330.6 10.9 %fusion.6 = f32[8,512,128]{2,1,0:T(8,128)S(1)} fusion(f32[8,512,128]{2,1,0:T(8,128)} %copy-done, f32[8,512,128]{2,1,0:T(8,128)} %bitcast.111, f32[8,512,512]{2,1,0:T(8,128)} %param.22), kind=kOutput, calls=%fused_computation.25 | convolution fusion | flops 3223322624 | bytes 14680064 | tf_op jit(solution)/shard_map/enm,emr->enr/dot_general | solution.py:127
  344.4 46.2 %all-reduce.13.cloned.1.call-done = f32[4096,128]{0,1:T(8,128)} async-done(((f32[4096,128]{0,1:T(8,128)}), f32[4096,128]{0,1:T(8,128)}) %all-reduce.13.cloned.1.call-update) | async-done | bytes 2097168 | tf_op jit(solution)/shard_map/psum | solution.py:125
  395.6 20.3 %all_to_all.31 = f32[32,32,128]{2,1,0:T(8,128)S(1)} all-to-all(f32[32,32,128]{2,1,0:T(8,128)S(1)} %broadcast_select_fusion.2), channel_id=1, replica_groups=mesh['row'=4,'col'=8] {'row','col'}, dimensions={0} | all-to-all | bytes 1048576 | tf_op jit(solution)/shard_map/all_to_all | solution.py:97
  417.0 36.1 %all-reduce.15.cloned.1.call-done = f32[2048,128]{0,1:T(8,128)} async-done(((f32[2048,128]{0,1:T(8,128)}), f32[2048,128]{0,1:T(8,128)}) %all-reduce.15.cloned.1.call-update) | async-done | bytes 1048592 | tf_op jit(solution)/shard_map/psum | solution.py:20
  453.1 39.1 %fusion.31 = f32[128,4096]{1,0:T(8,128)} fusion(f32[2048,128]{0,1:T(8,128)} %all-reduce.15.cloned.1.call-done, f32[4096,2048]{1,0:T(8,128)} %param.21), kind=kOutput, calls=%fused_computation.108 | convolution fusion | flops 12884901888 | bytes 36700160 | tf_op jit(solution)/shard_map/dot_general | solution.py:119
  500.2 4.6 all-to-all-start.5
  511.9 9.5 %all-to-all-done.5 = f32[32,32,128]{2,1,0:T(8,128)S(1)} async-done(((f32[32,32,128]{2,1,0:T(8,128)}), f32[32,32,128]{2,1,0:T(8,128)S(1)}, u32[]{:S(2)}, u32[]{:S(2)}) %all-to-all-start.5) | async-done | bytes 524320 | tf_op jit(solution)/shard_map/all_to_all | solution.py:100
  521.6 8.2 %scatter_custom_fusion.2 = f32[4096,128]{1,0:T(8,128)} fusion(s32[1024]{0:T(1024)S(1)} %bitcast.134, f32[1024,128]{1,0:T(8,128)S(1)} %bitcast.122, f32[]{:T(128)} %constant.143.clone.1), kind=kCustom, calls=%fused_computation.40 | custom fusion | flops 131072 | bytes 2097156 | tf_op jit(solution)/shard_map/scatter-add | solution.py:107
  529.8 10.7 %fusion.3 = f32[8,512,128]{2,1,0:T(8,128)} fusion(f32[8,512,128]{2,1,0:T(8,128)S(1)} %fusion.20, f32[8,512,128]{2,1,0:T(8,128)} %bitcast.110, f32[8,512,512]{2,1,0:T(8,128)} %param.22), kind=kOutput, calls=%fused_computation.21 | convolution fusion | flops 3223322624 | bytes 14680064 | tf_op jit(solution)/shard_map/enm,emr->enr/dot_general | solution.py:127
  542.2 47.5 %all-reduce.17.cloned.1.call-done = f32[4096,128]{0,1:T(8,128)} async-done(((f32[4096,128]{0,1:T(8,128)}), f32[4096,128]{0,1:T(8,128)}) %all-reduce.17.cloned.1.call-update) | async-done | bytes 2097168 | tf_op jit(solution)/shard_map/psum | solution.py:125
  (143 shorter events, 94.2 us)
Async XLA Ops:
  7.2 62.0 %all-reduce.7.cloned.1.call-start = ((), (), s32[]{:S(2)}) async-start(), calls=%async_computation.6 | async-start | bytes 2097152 | tf_op jit(solution)/shard_map/psum | solution.py:20
  10.1 2.5 copy-start.8
  10.1 2.5 copy-start.9
  10.1 5.5 copy-start.10
  10.1 6.9 %copy-start.1 = (f32[8,512,128]{2,1,0:T(8,128)S(1)}, f32[8,512,128]{2,1,0:T(8,128)}, u32[]{:S(2)}) copy-start(f32[8,512,128]{2,1,0:T(8,128)} %param.18) | copy-start | bytes 6291460
  19.8 13.8 %copy-start.7 = (f32[512,128]{1,0:T(8,128)S(1)}, f32[512,128]{1,0:T(8,128)}, u32[]{:S(2)}) copy-start(f32[512,128]{1,0:T(8,128)} %param.20) | copy-start | bytes 786436
  19.8 15.4 %copy-start.11 = (s32[16384]{0:T(1024)S(1)}, s32[16384]{0:T(1024)}, u32[]{:S(2)}) copy-start(s32[16384]{0:T(1024)} %param.26) | copy-start | bytes 196612
  20.9 23.9 %all-to-all-start = ((f32[32,32,128]{2,1,0:T(8,128)}), f32[32,32,128]{2,1,0:T(8,128)S(1)}, u32[]{:S(2)}, u32[]{:S(2)}) async-start(f32[32,32,128]{2,1,0:T(8,128)} %broadcast_select_fusion.8), calls=%async_computation | async-start | bytes 1048576 | tf_op jit(solution)/shard_map/all_to_all | solution.py:97
  28.9 92.0 %collective-permute-start = (f32[8,64,128]{2,1,0:T(8,128)}, f32[8,64,128]{2,1,0:T(8,128)S(1)}, u32[]{:S(2)}, u32[]{:S(2)}) collective-permute-start(f32[8,64,128]{2,1,0:T(8,128)} %slice.98), channel_id=1, source_target_pairs={{0,1},{1,2},{2,3},{3,4},{4,5},{5,6},{6,7},{7,8},{8,9},{9,10},{10,1... | collective-permute-start | bytes 786440 | tf_op jit(solution)/shard_map/ppermute | solution.py:15
  109.3 1.3 copy-start.5
  113.6 6.5 %copy-start.13 = (s32[8,64]{1,0:T(8,128)S(1)}, s32[8,64]{1,0:T(8,128)}, u32[]{:S(2)}) copy-start(s32[8,64]{1,0:T(8,128)} %param.27) | copy-start | bytes 6148
  114.6 20.9 %all-to-all-start.1 = ((f32[32,32,128]{2,1,0:T(8,128)}), f32[32,32,128]{2,1,0:T(8,128)S(1)}, u32[]{:S(2)}, u32[]{:S(2)}) async-start(f32[32,32,128]{2,1,0:T(8,128)} %broadcast_select_fusion.7), calls=%async_computation.1 | async-start | bytes 1048576 | tf_op jit(solution)/shard_map/all_to_all | solution.py:100
  119.2 72.0 %all-reduce.9.cloned.1.call-start = ((), (), s32[]{:S(2)}) async-start(), calls=%async_computation.7 | async-start | bytes 4194304 | tf_op jit(solution)/shard_map/psum | solution.py:125
  124.6 129.2 %all-reduce.11.cloned.1.call-start = ((), (), s32[]{:S(2)}) async-start(), calls=%async_computation.8 | async-start | bytes 2097152 | tf_op jit(solution)/shard_map/psum | solution.py:20
  155.0 150.7 %copy-start = (f32[8,512,128]{2,1,0:T(8,128)}, f32[8,512,128]{2,1,0:T(8,128)S(1)}, u32[]{:S(2)}) copy-start(f32[8,512,128]{2,1,0:T(8,128)S(1)} %fusion.21) | copy-start | bytes 6291460
  295.8 1.3 copy-start.6
  301.0 21.2 %all-to-all-start.3 = ((f32[32,32,128]{2,1,0:T(8,128)}), f32[32,32,128]{2,1,0:T(8,128)S(1)}, u32[]{:S(2)}, u32[]{:S(2)}) async-start(f32[32,32,128]{2,1,0:T(8,128)} %broadcast_select_fusion.4), calls=%async_computation.3 | async-start | bytes 1048576 | tf_op jit(solution)/shard_map/all_to_all | solution.py:100
  305.6 84.9 %all-reduce.13.cloned.1.call-start = ((), (), s32[]{:S(2)}) async-start(), calls=%async_computation.9 | async-start | bytes 4194304 | tf_op jit(solution)/shard_map/psum | solution.py:125
  305.7 3.3 collective-permute-start.1
  312.7 140.4 %all-reduce.15.cloned.1.call-start = ((), (), s32[]{:S(2)}) async-start(), calls=%async_computation.10 | async-start | bytes 2097152 | tf_op jit(solution)/shard_map/psum | solution.py:20
  393.0 1.3 copy-start.2
  500.2 21.2 %all-to-all-start.5 = ((f32[32,32,128]{2,1,0:T(8,128)}), f32[32,32,128]{2,1,0:T(8,128)S(1)}, u32[]{:S(2)}, u32[]{:S(2)}) async-start(f32[32,32,128]{2,1,0:T(8,128)} %broadcast_select_fusion.1), calls=%async_computation.5 | async-start | bytes 1048576 | tf_op jit(solution)/shard_map/all_to_all | solution.py:100
  504.8 84.9 %all-reduce.17.cloned.1.call-start = ((), (), s32[]{:S(2)}) async-start(), calls=%async_computation.11 | async-start | bytes 4194304 | tf_op jit(solution)/shard_map/psum | solution.py:125
  504.9 3.3 collective-permute-start.2
  (3 other events, 3.3 us)
Sparse Core Ops, SparseCore 0:
  12.7 56.4 all-reduce.6
  124.8 66.3 all-reduce.8
  196.2 57.6 all-reduce.10
  312.9 77.6 all-reduce.12
  395.5 57.5 all-reduce.14
  512.0 77.6 all-reduce.16
where the time goes:
time: 605 us; the launch traced here: 601 us
  waiting for transfers between devices  263 us (43%)
  matrix products  150 us (25%)
  other arithmetic  55 us (9%)
  local copies, waits for them, and re-layouts  49 us (8%)
  blocking collectives  40.9 us (7%)
  starting transfers between devices  28.6 us (5%)
  between operations  15.1 us (2%)
    psum x3, waiting for transfers between devices, shards(): residual = lax.psum(partial_value, 'col')  127 us
    dot_general x3, matrix products, shards(): jnp.dot(kernel, column_values, precision=highest, preferred_element_type=...  117 us
    psum x3, waiting for transfers between devices, spread(): return lax.psum(block, axis)  95.1 us
    all_to_all x2, blocking collectives, shards(): lax.all_to_all(outgoing, ('row', 'col'), split_axis=0, concat_axis=0, til...  40.9 us
    dot_general x3, matrix products, shards(): jnp.einsum('enm,emr->enr', elem_mats, volume_field, precision=highest)  32.8 us
    all_to_all x3, waiting for transfers between devices, shards(): lax.all_to_all(leaving, ('row', 'col'), split_axis=0, concat_axis=0, tile...  29.7 us
    scatter-add x3, other arithmetic, shards(): flux_field = jnp.zeros_like(volume_flat).at[flux_take.reshape(-1)].add(la...  24.3 us
    unnamed x35, local copies, waits for them, and re-layouts  15.8 us
  transfers between devices with their start and end apart: 13, of which 12 were waited for; matrix products, arithmetic and copies ran while one was open for 23% of the time, Pallas kernels for 0%

commit v1 on v0

--- a/solution.py
+++ b/solution.py
@@ -122,7 +122,11 @@
         row_start = col_index * share_rows
         own_part = lax.dynamic_slice_in_dim(partial_value, row_start, share_rows, 0) + local_term
         partial_value = lax.dynamic_update_slice_in_dim(partial_value, own_part, row_start, 0)
-        residual = lax.psum(partial_value, "col")
+        residual = partial_value
+        for hop in (1, 2, 4):
+            residual = residual + lax.ppermute(
+                residual, "col", [(dev, dev ^ hop) for dev in range(8)]
+            )
         panel_current = panel_current - boundary_step * residual
         applied = jnp.einsum("enm,emr->enr", elem_mats, volume_field, precision=highest)
         updated = volume_field - volume_step * (volume_field + applied - flux_field)

time: 605 us -> 855 us (1.41)
  the two profiles are of different devices: /device:TPU:0 before, /device:TPU:20 now
where the time goes in v1:
time: 855 us; the launch traced here: 846 us
  waiting for transfers between devices  492 us (58%)
  matrix products  149 us (17%)
  other arithmetic  71 us (8%)
  local copies, waits for them, and re-layouts  46.7 us (5%)
  starting transfers between devices  36.2 us (4%)
  blocking collectives  36 us (4%)
  between operations  14.7 us (2%)
    ppermute x9, waiting for transfers between devices, shards(): lax.ppermute(residual, 'col', [(dev, dev ^ hop) for dev in range(8)])  192 us
    ppermute x3, waiting for transfers between devices, passed_along(): return lax.ppermute(block, axis, route)  183 us
    dot_general x3, matrix products, shards(): jnp.dot(kernel, column_values, precision=highest, preferred_element_type=...  117 us
    psum x3, waiting for transfers between devices, spread(): return lax.psum(block, axis)  104 us
    all_to_all x2, blocking collectives, shards(): lax.all_to_all(outgoing, ('row', 'col'), split_axis=0, concat_axis=0, til...  36 us
    dot_general x3, matrix products, shards(): jnp.einsum('enm,emr->enr', elem_mats, volume_field, precision=highest)  31.9 us
    scatter-add x3, other arithmetic, shards(): flux_field = jnp.zeros_like(volume_flat).at[flux_take.reshape(-1)].add(la...  24 us
  transfers between devices with their start and end apart: 19, of which 13 were waited for; matrix products, arithmetic and copies ran while one was open for 14% of the time, Pallas kernels for 0%

profile of v1, /device:TPU:20, one launch (start us, length us, event | category | flops | bytes accessed | tf_op | source)
XLA Modules:
  0.0 846.1 jit_solution(123039404420790050)
XLA Ops:
  20.9 5.9 all-to-all-start
  27.3 12.6 %all-to-all-done = f32[32,32,128]{2,1,0:T(8,128)S(1)} async-done(((f32[32,32,128]{2,1,0:T(8,128)}), f32[32,32,128]{2,1,0:T(8,128)S(1)}, u32[]{:S(2)}, u32[]{:S(2)}) %all-to-all-start) | async-done | bytes 524320 | tf_op jit(solution)/shard_map/all_to_all | solution.py:97
  41.1 26.3 %all-reduce.4.cloned.1.call-done = f32[2048,128]{0,1:T(8,128)} async-done(((f32[2048,128]{0,1:T(8,128)}), f32[2048,128]{0,1:T(8,128)}) %all-reduce.4.cloned.1.call-update) | async-done | bytes 1048592 | tf_op jit(solution)/shard_map/psum | solution.py:20
  67.4 39.2 %fusion.29 = f32[128,4096]{1,0:T(8,128)} fusion(f32[2048,128]{0,1:T(8,128)} %all-reduce.4.cloned.1.call-done, f32[4096,2048]{1,0:T(8,128)} %param.21), kind=kOutput, calls=%fused_computation.106 | convolution fusion | flops 12884901888 | bytes 36700160 | tf_op jit(solution)/shard_map/dot_general | solution.py:119
  126.7 6.0 all-to-all-start.1
  132.7 33.5 %collective-permute-done.1 = f32[4096,128]{0,1:T(8,128)} collective-permute-done((f32[4096,128]{0,1:T(8,128)}, f32[4096,128]{0,1:T(8,128)}, u32[]{:S(2)}, u32[]{:S(2)}) %collective-permute-start.1) | collective-permute-done | bytes 2097184 | tf_op jit(solution)/shard_map/ppermute | solution.py:127
  170.1 4.4 collective-permute-start.2
  179.9 7.9 scatter_custom_fusion
  187.8 11.1 %multiply_subtract_fusion.2 = f32[8,512,128]{2,1,0:T(8,128)S(1)} fusion(f32[8,512,128]{2,1,0:T(8,128)} %param.18, f32[8,512,128]{2,1,0:T(8,128)} %bitcast.112, f32[8,512,512]{2,1,0:T(8,128)} %param.22), kind=kOutput, calls=%fused_computation.28 | convolution fusion | flops 3223322624 | bytes 14680064 | tf_op jit(solution)/shard_map/enm,emr->enr/dot_general | solution.py:131
  201.8 60.7 %collective-permute-done.2 = f32[4096,128]{0,1:T(8,128)} collective-permute-done((f32[4096,128]{0,1:T(8,128)}, f32[4096,128]{0,1:T(8,128)}, u32[]{:S(2)}, u32[]{:S(2)}) %collective-permute-start.2) | collective-permute-done | bytes 2097184 | tf_op jit(solution)/shard_map/ppermute | solution.py:127
  268.4 19.0 %all_to_all.30 = f32[32,32,128]{2,1,0:T(8,128)S(1)} all-to-all(f32[32,32,128]{2,1,0:T(8,128)S(1)} %broadcast_select_fusion.5), channel_id=1, replica_groups=mesh['row'=4,'col'=8] {'row','col'}, dimensions={0} | all-to-all | bytes 1048576 | tf_op jit(solution)/shard_map/all_to_all | solution.py:97
  288.6 38.8 %all-reduce.6.cloned.1.call-done = f32[2048,128]{0,1:T(8,128)} async-done(((f32[2048,128]{0,1:T(8,128)}), f32[2048,128]{0,1:T(8,128)}) %all-reduce.6.cloned.1.call-update) | async-done | bytes 1048592 | tf_op jit(solution)/shard_map/psum | solution.py:20
  327.4 39.1 %fusion.30 = f32[128,4096]{1,0:T(8,128)} fusion(f32[2048,128]{0,1:T(8,128)} %all-reduce.6.cloned.1.call-done, f32[4096,2048]{1,0:T(8,128)} %param.21), kind=kOutput, calls=%fused_computation.107 | convolution fusion | flops 12884901888 | bytes 36700160 | tf_op jit(solution)/shard_map/dot_general | solution.py:119
  384.5 42.7 %collective-permute-done.5 = f32[4096,128]{0,1:T(8,128)} collective-permute-done((f32[4096,128]{0,1:T(8,128)}, f32[4096,128]{0,1:T(8,128)}, u32[]{:S(2)}, u32[]{:S(2)}) %collective-permute-start.5) | collective-permute-done | bytes 2097184 | tf_op jit(solution)/shard_map/ppermute | solution.py:127
  433.6 91.6 %collective-permute-done.7 = f32[8,64,128]{2,1,0:T(8,128)S(1)} collective-permute-done((f32[8,64,128]{2,1,0:T(8,128)S(1)}, f32[8,64,128]{2,1,0:T(8,128)S(1)}, u32[]{:S(2)}, u32[]{:S(2)}) %collective-permute-start.7) | collective-permute-done | bytes 262176 | tf_op jit(solution)/shard_map/ppermute | solution.py:15
  529.1 8.0 scatter_custom_fusion.1
  537.2 10.9 %fusion.6 = f32[8,512,128]{2,1,0:T(8,128)S(1)} fusion(f32[8,512,128]{2,1,0:T(8,128)} %copy-done, f32[8,512,128]{2,1,0:T(8,128)} %bitcast.111, f32[8,512,512]{2,1,0:T(8,128)} %param.22), kind=kOutput, calls=%fused_computation.25 | convolution fusion | flops 3223322624 | bytes 14680064 | tf_op jit(solution)/shard_map/enm,emr->enr/dot_general | solution.py:131
  556.8 16.9 %all_to_all.31 = f32[32,32,128]{2,1,0:T(8,128)S(1)} all-to-all(f32[32,32,128]{2,1,0:T(8,128)S(1)} %broadcast_select_fusion.2), channel_id=1, replica_groups=mesh['row'=4,'col'=8] {'row','col'}, dimensions={0} | all-to-all | bytes 1048576 | tf_op jit(solution)/shard_map/all_to_all | solution.py:97
  574.9 38.8 %all-reduce.8.cloned.1.call-done = f32[2048,128]{0,1:T(8,128)} async-done(((f32[2048,128]{0,1:T(8,128)}), f32[2048,128]{0,1:T(8,128)}) %all-reduce.8.cloned.1.call-update) | async-done | bytes 1048592 | tf_op jit(solution)/shard_map/psum | solution.py:20
  613.7 39.2 %fusion.31 = f32[128,4096]{1,0:T(8,128)} fusion(f32[2048,128]{0,1:T(8,128)} %all-reduce.8.cloned.1.call-done, f32[4096,2048]{1,0:T(8,128)} %param.21), kind=kOutput, calls=%fused_computation.108 | convolution fusion | flops 12884901888 | bytes 36700160 | tf_op jit(solution)/shard_map/dot_general | solution.py:119
  670.8 42.8 %collective-permute-done.9 = f32[4096,128]{0,1:T(8,128)} collective-permute-done((f32[4096,128]{0,1:T(8,128)}, f32[4096,128]{0,1:T(8,128)}, u32[]{:S(2)}, u32[]{:S(2)}) %collective-permute-start.9) | collective-permute-done | bytes 2097184 | tf_op jit(solution)/shard_map/ppermute | solution.py:127
  719.9 91.6 %collective-permute-done.11 = f32[8,64,128]{2,1,0:T(8,128)S(1)} collective-permute-done((f32[8,64,128]{2,1,0:T(8,128)S(1)}, f32[8,64,128]{2,1,0:T(8,128)S(1)}, u32[]{:S(2)}, u32[]{:S(2)}) %collective-permute-start.11) | collective-permute-done | bytes 262176 | tf_op jit(solution)/shard_map/ppermute | solution.py:15
  815.5 8.1 scatter_custom_fusion.2
  823.5 9.9 %fusion.3 = f32[8,512,128]{2,1,0:T(8,128)S(1)} fusion(f32[8,512,128]{2,1,0:T(8,128)S(1)} %fusion.20, f32[8,512,128]{2,1,0:T(8,128)} %bitcast.110, f32[8,512,512]{2,1,0:T(8,128)} %param.22), kind=kOutput, calls=%fused_computation.21 | convolution fusion | flops 3223322624 | bytes 14680064 | tf_op jit(solution)/shard_map/enm,emr->enr/dot_general | solution.py:131
  (156 shorter events, 126.1 us)
Async XLA Ops:
  7.2 60.3 %all-reduce.4.cloned.1.call-start = ((), (), s32[]{:S(2)}) async-start(), calls=%async_computation.6 | async-start | bytes 2097152 | tf_op jit(solution)/shard_map/psum | solution.py:20
  19.9 6.9 copy-start.6
  20.9 19.0 %all-to-all-start = ((f32[32,32,128]{2,1,0:T(8,128)}), f32[32,32,128]{2,1,0:T(8,128)S(1)}, u32[]{:S(2)}, u32[]{:S(2)}) async-start(f32[32,32,128]{2,1,0:T(8,128)} %broadcast_select_fusion.8), calls=%async_computation | async-start | bytes 1048576 | tf_op jit(solution)/shard_map/all_to_all | solution.py:97
  109.3 12.6 %copy-start.10 = (s32[16384]{0:T(1024)S(1)}, s32[16384]{0:T(1024)}, u32[]{:S(2)}) copy-start(s32[16384]{0:T(1024)} %param.26) | copy-start | bytes 196612
  109.3 4.2 collective-permute-start
  115.1 51.2 %collective-permute-start.1 = (f32[4096,128]{0,1:T(8,128)}, f32[4096,128]{0,1:T(8,128)}, u32[]{:S(2)}, u32[]{:S(2)}) collective-permute-start(f32[4096,128]{0,1:T(8,128)} %add.193), channel_id=1, source_target_pairs={{0,2},{1,3},{2,0},{3,1},{4,6},{5,7},{6,4},{7,5},{8,10},{9,11},{10,... | collective-permute-start | bytes 6291464 | tf_op jit(solution)/shard_map/ppermute | solution.py:127
  116.6 59.3 %collective-permute-start.3 = (f32[8,64,128]{2,1,0:T(8,128)S(1)}, f32[8,64,128]{2,1,0:T(8,128)S(1)}, u32[]{:S(2)}, u32[]{:S(2)}) collective-permute-start(f32[8,64,128]{2,1,0:T(8,128)S(1)} %slice.98), channel_id=1, source_target_pairs={{0,1},{1,2},{2,3},{3,4},{4,5},{5,6},{6,7},{7,8},{8,9},{9,10},{10,1... | collective-permute-start | bytes 786440 | tf_op jit(solution)/shard_map/ppermute | solution.py:15
  126.7 53.0 %all-to-all-start.1 = ((f32[32,32,128]{2,1,0:T(8,128)}), f32[32,32,128]{2,1,0:T(8,128)S(1)}, u32[]{:S(2)}, u32[]{:S(2)}) async-start(f32[32,32,128]{2,1,0:T(8,128)} %broadcast_select_fusion.7), calls=%async_computation.1 | async-start | bytes 1048576 | tf_op jit(solution)/shard_map/all_to_all | solution.py:100
  132.7 42.4 %copy-start.12 = (s32[8,64]{1,0:T(8,128)S(1)}, s32[8,64]{1,0:T(8,128)}, u32[]{:S(2)}) copy-start(s32[8,64]{1,0:T(8,128)} %param.27) | copy-start | bytes 6148
  132.7 194.7 %all-reduce.6.cloned.1.call-start = ((), (), s32[]{:S(2)}) async-start(), calls=%async_computation.7 | async-start | bytes 2097152 | tf_op jit(solution)/shard_map/psum | solution.py:20
  170.1 92.5 %collective-permute-start.2 = (f32[4096,128]{0,1:T(8,128)}, f32[4096,128]{0,1:T(8,128)}, u32[]{:S(2)}, u32[]{:S(2)}) collective-permute-start(f32[4096,128]{0,1:T(8,128)} %add.194), channel_id=1, source_target_pairs={{0,4},{1,5},{2,6},{3,7},{4,0},{5,1},{6,2},{7,3},{8,12},{9,13},{10,... | collective-permute-start | bytes 6291464 | tf_op jit(solution)/shard_map/ppermute | solution.py:127
  199.0 232.7 %copy-start = (f32[8,512,128]{2,1,0:T(8,128)}, f32[8,512,128]{2,1,0:T(8,128)S(1)}, u32[]{:S(2)}) copy-start(f32[8,512,128]{2,1,0:T(8,128)S(1)} %fusion.21) | copy-start | bytes 6291460
  369.3 4.2 collective-permute-start.4
  375.0 52.2 %collective-permute-start.5 = (f32[4096,128]{0,1:T(8,128)}, f32[4096,128]{0,1:T(8,128)}, u32[]{:S(2)}, u32[]{:S(2)}) collective-permute-start(f32[4096,128]{0,1:T(8,128)} %add.202), channel_id=1, source_target_pairs={{0,2},{1,3},{2,0},{3,1},{4,6},{5,7},{6,4},{7,5},{8,10},{9,11},{10,... | collective-permute-start | bytes 6291464 | tf_op jit(solution)/shard_map/ppermute | solution.py:127
  380.5 148.5 %all-to-all-start.3 = ((f32[32,32,128]{2,1,0:T(8,128)}), f32[32,32,128]{2,1,0:T(8,128)S(1)}, u32[]{:S(2)}, u32[]{:S(2)}) async-start(f32[32,32,128]{2,1,0:T(8,128)} %broadcast_select_fusion.4), calls=%async_computation.3 | async-start | bytes 1048576 | tf_op jit(solution)/shard_map/all_to_all | solution.py:100
  384.5 229.2 %all-reduce.8.cloned.1.call-start = ((), (), s32[]{:S(2)}) async-start(), calls=%async_computation.8 | async-start | bytes 2097152 | tf_op jit(solution)/shard_map/psum | solution.py:20
  431.1 119.9 %collective-permute-start.6 = (f32[4096,128]{0,1:T(8,128)}, f32[4096,128]{0,1:T(8,128)}, u32[]{:S(2)}, u32[]{:S(2)}) collective-permute-start(f32[4096,128]{0,1:T(8,128)} %add.203), channel_id=1, source_target_pairs={{0,4},{1,5},{2,6},{3,7},{4,0},{5,1},{6,2},{7,3},{8,12},{9,13},{10,... | collective-permute-start | bytes 6291464 | tf_op jit(solution)/shard_map/ppermute | solution.py:127
  431.7 93.5 %collective-permute-start.7 = (f32[8,64,128]{2,1,0:T(8,128)S(1)}, f32[8,64,128]{2,1,0:T(8,128)S(1)}, u32[]{:S(2)}, u32[]{:S(2)}) collective-permute-start(f32[8,64,128]{2,1,0:T(8,128)S(1)} %slice.131), channel_id=1, source_target_pairs={{0,1},{1,2},{2,3},{3,4},{4,5},{5,6},{6,7},{7,8},{8,9},{9,10},{10,1... | collective-permute-start | bytes 786440 | tf_op jit(solution)/shard_map/ppermute | solution.py:15
  655.6 4.2 collective-permute-start.8
  661.3 52.2 %collective-permute-start.9 = (f32[4096,128]{0,1:T(8,128)}, f32[4096,128]{0,1:T(8,128)}, u32[]{:S(2)}, u32[]{:S(2)}) collective-permute-start(f32[4096,128]{0,1:T(8,128)} %add.208), channel_id=1, source_target_pairs={{0,2},{1,3},{2,0},{3,1},{4,6},{5,7},{6,4},{7,5},{8,10},{9,11},{10,... | collective-permute-start | bytes 6291464 | tf_op jit(solution)/shard_map/ppermute | solution.py:127
  666.8 148.5 %all-to-all-start.5 = ((f32[32,32,128]{2,1,0:T(8,128)}), f32[32,32,128]{2,1,0:T(8,128)S(1)}, u32[]{:S(2)}, u32[]{:S(2)}) async-start(f32[32,32,128]{2,1,0:T(8,128)} %broadcast_select_fusion.1), calls=%async_computation.5 | async-start | bytes 1048576 | tf_op jit(solution)/shard_map/all_to_all | solution.py:100
  717.4 117.5 %collective-permute-start.10 = (f32[4096,128]{0,1:T(8,128)}, f32[4096,128]{0,1:T(8,128)}, u32[]{:S(2)}, u32[]{:S(2)}) collective-permute-start(f32[4096,128]{0,1:T(8,128)} %add.209), channel_id=1, source_target_pairs={{0,4},{1,5},{2,6},{3,7},{4,0},{5,1},{6,2},{7,3},{8,12},{9,13},{10,... | collective-permute-start | bytes 6291464 | tf_op jit(solution)/shard_map/ppermute | solution.py:127
  718.0 93.5 %collective-permute-start.11 = (f32[8,64,128]{2,1,0:T(8,128)S(1)}, f32[8,64,128]{2,1,0:T(8,128)S(1)}, u32[]{:S(2)}, u32[]{:S(2)}) collective-permute-start(f32[8,64,128]{2,1,0:T(8,128)S(1)} %slice.133), channel_id=1, source_target_pairs={{0,1},{1,2},{2,3},{3,4},{4,5},{5,6},{6,7},{7,8},{8,9},{9,10},{10,1... | collective-permute-start | bytes 786440 | tf_op jit(solution)/shard_map/ppermute | solution.py:15
  823.5 11.4 %copy-start.3 = (f32[4096,128]{0,1:T(8,128)S(1)}, f32[4096,128]{0,1:T(8,128)}, u32[]{:S(2)}) copy-start(f32[4096,128]{0,1:T(8,128)} %copy-done.2) | copy-start | bytes 6291460
  (8 other events, 23.0 us)
Sparse Core Ops, SparseCore 0:
  12.7 54.6 all-reduce.3
  268.3 59.0 all-reduce.5
  556.7 56.9 all-reduce.7
